TPU v7x, 512 devices: a whole 4x4x16 slice. The times are simulated.
512 devices in a mesh: wide: 64 (over z, y_hi, core), narrow: 8 (over x, y_lo).
Axes of the slice: x: 4, y: 4 (y_hi: 2, y_lo: 2; y = y_hi * 2 + y_lo), z: 16, core: 2. Of those that a mesh axis runs over, the one named last changes fastest.
Arguments:
- tokens: bfloat16 [512, 8192], P('wide', 'narrow'), may hold values from -6 to 6
- cotangent: bfloat16 [512, 8192], P('wide', 'narrow'), may hold values from -2.390625 to 2.390625
- gate_vals: bfloat16 [8, 64, 12, 128, 128], P('narrow', 'wide'), may hold values from -0.125 to 0.125
- up_vals: bfloat16 [8, 64, 12, 128, 128], P('narrow', 'wide'), may hold values from -0.125 to 0.125
- gu_index: int32 [8, 64, 12], P('narrow', 'wide'), may hold values from 0 to 15, as said below
- gu_count: int32 [8, 64], P('narrow', 'wide'), may hold values from 1 to 12, as said below
- down_vals: bfloat16 [64, 8, 12, 128, 128], P('wide', 'narrow'), may hold values from -0.09375 to 0.09375
- down_index: int32 [64, 8, 12], P('wide', 'narrow'), may hold values from 0 to 15, as said below
- down_count: int32 [64, 8], P('wide', 'narrow'), may hold values from 1 to 12, as said below
Outputs:
- d_tokens: bfloat16 [512, 8192], P('wide', 'narrow')
- gate_grad: bfloat16 [8, 64, 12, 128, 128], P('narrow', 'wide')
- up_grad: bfloat16 [8, 64, 12, 128, 128], P('narrow', 'wide')
- down_grad: bfloat16 [64, 8, 12, 128, 128], P('wide', 'narrow')
Inputs may be any that keep to these rules, and one draw needn't show every extreme that they name: `gu_index`: within each tile all 12 entries are different. `gu_count`: some tile has exactly 12 live slots. `down_index`: within each tile all 12 entries are different. `down_count`: some tile has exactly 12 live slots.
All inputs are finite; a program needn't handle non-finite values.
Results may differ from a plain program's by a relative error of at most 0.005.
Values may be sent and summed in bfloat16 or wider, within the bound.
A program may use at most 64 MiB of HBM per device.

v0:
```python
import jax
import jax.numpy as jnp
from jax import lax
from jax.sharding import PartitionSpec as P

FF = 16384


def apply_blocks(inputs, tile_values, source_blocks, target_blocks, target_total, form):
    block_size = tile_values.shape[-1]
    row_total = inputs.shape[0]
    pieces = inputs.reshape(row_total, inputs.shape[1] // block_size, block_size)
    picked = jnp.take(pieces, source_blocks, axis=1)
    products = jnp.einsum(form, picked, tile_values, preferred_element_type=jnp.float32)
    placer = (target_blocks[:, None] == jnp.arange(target_total, dtype=jnp.int32)[None, :]).astype(
        jnp.float32
    )
    placed = jnp.einsum("rsn,sc->rcn", products, placer, precision=lax.Precision.HIGHEST)
    return placed.reshape(row_total, target_total * block_size)


def block_grads(left, right, left_blocks, right_blocks, alive, block_size):
    row_total = left.shape[0]
    left_parts = jnp.take(
        left.reshape(row_total, left.shape[1] // block_size, block_size), left_blocks, axis=1
    )
    right_parts = jnp.take(
        right.reshape(row_total, right.shape[1] // block_size, block_size), right_blocks, axis=1
    )
    result = jnp.einsum("rsk,rsn->skn", left_parts, right_parts, preferred_element_type=jnp.float32)
    return jnp.where(alive[:, None, None], result, 0.0).astype(jnp.bfloat16)


def on_device(
    tokens, cotangent, gate_vals, up_vals, gu_index, gu_count, down_vals, down_index, down_count
):
    block_size = gate_vals.shape[-1]
    slots_total = gate_vals.shape[2]
    wide_size = lax.axis_size("wide")
    d_blocks = tokens.shape[1] // block_size
    f_blocks = FF // (block_size * wide_size)
    f_width = f_blocks * block_size
    slot_range = jnp.arange(slots_total, dtype=jnp.int32)
    gate_alive = slot_range < gu_count[0, 0]
    down_alive = slot_range < down_count[0, 0]
    gate_rows = gu_index[0, 0] // f_blocks
    gate_cols = gu_index[0, 0] % f_blocks
    down_rows = down_index[0, 0] // d_blocks
    down_cols = down_index[0, 0] % d_blocks
    gate_tile = jnp.where(gate_alive[:, None, None], gate_vals[0, 0], 0)
    up_tile = jnp.where(gate_alive[:, None, None], up_vals[0, 0], 0)
    down_tile = jnp.where(down_alive[:, None, None], down_vals[0, 0], 0)
    paired = jnp.concatenate([gate_tile, up_tile], axis=0)
    paired_rows = jnp.concatenate([gate_rows, gate_rows], axis=0)
    paired_cols = jnp.concatenate([gate_cols, gate_cols + f_blocks], axis=0)
    paired_alive = jnp.concatenate([gate_alive, gate_alive], axis=0)
    x_all = lax.all_gather(tokens, "wide", axis=0, tiled=True)
    dy_all = lax.all_gather(cotangent, "wide", axis=0, tiled=True)
    merged = lax.psum_scatter(
        apply_blocks(x_all, paired, paired_rows, paired_cols, 2 * f_blocks, "rsk,skn->rsn"),
        "narrow",
        scatter_dimension=0,
        tiled=True,
    )
    d_hidden = lax.psum_scatter(
        apply_blocks(dy_all, down_tile, down_cols, down_rows, f_blocks, "rsn,skn->rsk"),
        "narrow",
        scatter_dimension=0,
        tiled=True,
    )
    gate_out = merged[:, :f_width]
    up_out = merged[:, f_width:]
    sigmoid_g = jax.nn.sigmoid(gate_out)
    hidden = (gate_out * sigmoid_g * up_out).astype(jnp.bfloat16)
    d_gate = (d_hidden * up_out * sigmoid_g * (1.0 + gate_out * (1.0 - sigmoid_g))).astype(
        jnp.bfloat16
    )
    d_up = (d_hidden * gate_out * sigmoid_g).astype(jnp.bfloat16)
    hidden_all, dgate_all, dup_all = (
        lax.all_gather(hidden, "narrow", axis=0, tiled=True),
        lax.all_gather(d_gate, "narrow", axis=0, tiled=True),
        lax.all_gather(d_up, "narrow", axis=0, tiled=True),
    )
    down_grad = block_grads(hidden_all, dy_all, down_rows, down_cols, down_alive, block_size)
    grads_pair = jnp.concatenate([dgate_all, dup_all], axis=1)
    both_grads = block_grads(x_all, grads_pair, paired_rows, paired_cols, paired_alive, block_size)
    gate_grad = both_grads[:slots_total]
    up_grad = both_grads[slots_total:]
    d_tokens = lax.psum_scatter(
        apply_blocks(grads_pair, paired, paired_cols, paired_rows, d_blocks, "rsn,skn->rsk"),
        "wide",
        scatter_dimension=0,
        tiled=True,
    ).astype(jnp.bfloat16)
    return (d_tokens, gate_grad[None, None], up_grad[None, None], down_grad[None, None])


def solution(mesh):
    in_specs = (
        P("wide", "narrow"),
        P("wide", "narrow"),
        P("narrow", "wide", None, None, None),
        P("narrow", "wide", None, None, None),
        P("narrow", "wide", None),
        P("narrow", "wide"),
        P("wide", "narrow", None, None, None),
        P("wide", "narrow", None),
        P("wide", "narrow"),
    )
    out_specs = (
        P("wide", "narrow"),
        P("narrow", "wide", None, None, None),
        P("narrow", "wide", None, None, None),
        P("wide", "narrow", None, None, None),
    )
    return jax.shard_map(
        on_device, mesh=mesh, in_specs=in_specs, out_specs=out_specs, check_vma=False
    )
```

profile of v0, /device:TPU:6, one launch (start us, length us, event | category | flops | bytes accessed | tf_op | source)
XLA Modules:
  0.0 692.6 jit_solution(14160900754381156844)
XLA Ops:
  10.0 1.2 copy.61
  11.2 1.2 copy.62
  12.4 1.9 copy.63
  15.5 1.2 broadcast_add_fusion
  17.7 139.1 %all-gather.3.cloned.1.call-done = bf16[512,1024]{1,0:T(8,128)(2,1)} async-done(((bf16[8,1024]{1,0:T(8,128)(2,1)}), bf16[512,1024]{1,0:T(8,128)(2,1)}) %all-gather.3.cloned.1.call-update) | async-done | bytes 1048592 | tf_op jit(solution)/shard_map/all_gather | solution.py:58
  156.7 1.5 copy.64
  158.9 1.9 gather_fusion.1
  160.9 2.3 convolution_bitcast_fusion
  163.2 3.5 copy.67
  166.7 3.8 convolution_bitcast_fusion.2
  171.9 124.8 %all-gather.5.cloned.1.call-done = bf16[512,1024]{1,0:T(8,128)(2,1)} async-done(((bf16[8,1024]{1,0:T(8,128)(2,1)}), bf16[512,1024]{1,0:T(8,128)(2,1)}) %all-gather.5.cloned.1.call-update) | async-done | bytes 1048592 | tf_op jit(solution)/shard_map/all_gather | solution.py:57
  296.7 1.5 copy.69
  298.9 2.7 gather_fusion.2
  301.5 5.6 fusion.7
  307.2 6.6 copy.71
  313.8 5.1 convolution_bitcast_fusion.1
  319.3 1.3 copy.97
  320.7 18.1 %reduce-scatter.10.cloned.1.call-done = f32[64,256]{1,0:T(8,128)} async-done(((f32[512,256]{1,0:T(8,128)}), f32[64,256]{1,0:T(8,128)}) %reduce-scatter.10.cloned.1.call-update) | async-done | bytes 65552 | tf_op jit(solution)/shard_map/reduce_scatter | solution.py:65
  338.8 48.9 %reduce-scatter.12.cloned.1.call-done = f32[64,512]{1,0:T(8,128)} async-done(((f32[512,512]{1,0:T(8,128)}), f32[64,512]{1,0:T(8,128)}) %reduce-scatter.12.cloned.1.call-update) | async-done | bytes 131088 | tf_op jit(solution)/shard_map/reduce_scatter | solution.py:59
  388.7 28.4 %all_gather.17 = bf16[512,256]{1,0:T(8,128)(2,1)S(1)} all-gather(bf16[64,256]{1,0:T(8,128)(2,1)S(1)} %get-tuple-element.31), channel_id=1, replica_groups=mesh['wide'=64,'narrow'=8] {'narrow'}, dimensions={0}, use_global_device_ids=true | all-gather | bytes 294912 | tf_op jit(solution)/shard_map/all_gather | solution.py:81
  417.2 28.6 %all_gather.18 = bf16[512,256]{1,0:T(8,128)(2,1)S(1)} all-gather(bf16[64,256]{1,0:T(8,128)(2,1)S(1)} %get-tuple-element.32), channel_id=1, replica_groups=mesh['wide'=64,'narrow'=8] {'narrow'}, dimensions={0}, use_global_device_ids=true | all-gather | bytes 294912 | tf_op jit(solution)/shard_map/all_gather | solution.py:82
  446.2 2.7 gather_fusion.3
  448.9 5.7 fusion.10
  454.6 6.6 copy.81
  461.1 4.3 fusion.42
  465.5 1.8 copy.101
  467.9 28.4 %all_gather.19 = bf16[512,256]{1,0:T(8,128)(2,1)S(1)} all-gather(bf16[64,256]{1,0:T(8,128)(2,1)S(1)} %get-tuple-element.33), channel_id=1, replica_groups=mesh['wide'=64,'narrow'=8] {'narrow'}, dimensions={0}, use_global_device_ids=true | all-gather | bytes 294912 | tf_op jit(solution)/shard_map/all_gather | solution.py:80
  496.6 1.9 gather_fusion
  498.6 2.8 fusion.33
  502.4 3.2 select_convert_fusion
  506.6 178.1 %reduce-scatter.8.cloned.1.call-done = f32[8,1024]{1,0:T(8,128)} async-done(((f32[512,1024]{1,0:T(8,128)}), f32[8,1024]{1,0:T(8,128)}) %reduce-scatter.8.cloned.1.call-update) | async-done | bytes 32784 | tf_op jit(solution)/shard_map/reduce_scatter | solution.py:89
  684.7 1.4 convert_element_type.27
  (52 shorter events, 11.1 us)
Async XLA Ops:
  7.2 149.6 %all-gather.3.cloned.1.call-start = ((), (), s32[]{:S(2)}) async-start(), calls=%async_computation.3 | async-start | bytes 1064960 | tf_op jit(solution)/shard_map/all_gather | solution.py:58
  7.9 288.8 %all-gather.5.cloned.1.call-start = ((), (), s32[]{:S(2)}) async-start(), calls=%async_computation.4 | async-start | bytes 1064960 | tf_op jit(solution)/shard_map/all_gather | solution.py:57
  8.6 330.1 %reduce-scatter.10.cloned.1.call-start = ((), (), s32[]{:S(2)}) async-start(), calls=%async_computation.6 | async-start | bytes 589824 | tf_op jit(solution)/shard_map/reduce_scatter | solution.py:65
  14.4 146.5 %copy-start.5 = (pred[12]{0:T(512)(128)(4,1)}, pred[12]{0:T(512)(128)(4,1)S(1)}, u32[]{:S(2)}) copy-start(pred[12]{0:T(512)(128)(4,1)S(1)} %iota_compare_fusion.3) | copy-start | bytes 40
  166.7 5.1 copy-start.2
  166.7 5.1 copy-start.3
  166.7 5.1 copy-start.4
  171.7 216.0 %reduce-scatter.12.cloned.1.call-start = ((), (), s32[]{:S(2)}) async-start(), calls=%async_computation.7 | async-start | bytes 1179648 | tf_op jit(solution)/shard_map/reduce_scatter | solution.py:59
  298.8 2.7 copy-start.1
  320.6 364.1 %reduce-scatter.8.cloned.1.call-start = ((), (), s32[]{:S(2)}) async-start(), calls=%async_computation.5 | async-start | bytes 2129920 | tf_op jit(solution)/shard_map/reduce_scatter | solution.py:89
  465.5 1.9 copy-start.6
  465.5 2.4 copy-start.7
  498.6 3.8 copy-start
Sparse Core Ops, SparseCore 0:
  11.3 145.4 all-gather.2
  160.0 136.5 all-gather.4
  299.5 39.2 reduce-scatter.9
  341.5 46.1 reduce-scatter.11
  467.4 217.1 reduce-scatter.7
where the time goes:
time: 693 us
  waiting for transfers between devices  510 us (74%)
  blocking collectives  85.3 us (12%)
  local copies, waits for them, and re-layouts  42.1 us (6%)
  matrix products  32.8 us (5%)
  between operations  15.3 us (2%)
    reduce_scatter x1, waiting for transfers between devices, on_device(): lax.psum_scatter(apply_blocks(grads_pair, paired, paired_cols, paired_row...  178 us
    all_gather x1, waiting for transfers between devices, on_device(): dy_all = lax.all_gather(cotangent, 'wide', axis=0, tiled=True)  139 us
    all_gather x1, waiting for transfers between devices, on_device(): x_all = lax.all_gather(tokens, 'wide', axis=0, tiled=True)  125 us
    reduce_scatter x1, waiting for transfers between devices, on_device(): lax.psum_scatter(apply_blocks(x_all, paired, paired_rows, paired_cols, 2...  48.9 us
    all_gather x1, blocking collectives, on_device(): lax.all_gather(d_up, 'narrow', axis=0, tiled=True)  28.6 us
    all_gather x1, blocking collectives, on_device(): lax.all_gather(hidden, 'narrow', axis=0, tiled=True)  28.4 us
    all_gather x1, blocking collectives, on_device(): lax.all_gather(d_gate, 'narrow', axis=0, tiled=True)  28.4 us
    reduce_scatter x1, waiting for transfers between devices, on_device(): lax.psum_scatter(apply_blocks(dy_all, down_tile, down_cols, down_rows, f_...  18.1 us
  transfers between devices with their start and end apart: 5, of which 5 were waited for; matrix products, arithmetic and copies ran while one was open for 8% of the time, Pallas kernels for 0%

commit v1 on v0

v1 whole, which is shorter than its diff:
```python
import jax
import jax.numpy as jnp
from jax import lax
from jax.experimental import pallas as pl
from jax.experimental.pallas import tpu as pltpu
from jax.sharding import PartitionSpec as P

MESH = pl.DeviceIdType.MESH
VMEM = pl.BlockSpec(memory_space=pltpu.VMEM)
SMEM = pl.BlockSpec(memory_space=pltpu.SMEM)
F32 = jnp.float32
BF16 = jnp.bfloat16

Z = 16
N = 8
B = 128


def wide_place():
    w = lax.axis_index("wide")
    return w // 4, (w // 2) % 2, w % 2


def wide_at(z, y, c):
    return ((z + Z) % Z * 2 + y) * 2 + c


def greet(axis, peers):
    barrier = pltpu.get_barrier_semaphore()
    for peer in peers:
        pl.semaphore_signal(barrier, inc=1, device_id={axis: peer}, device_id_type=MESH)
    pl.semaphore_wait(barrier, len(peers))


def send(axis, peer, src, dst, send_sem, recv_sem):
    copy = pltpu.make_async_remote_copy(
        src_ref=src,
        dst_ref=dst,
        send_sem=send_sem,
        recv_sem=recv_sem,
        device_id={axis: peer},
        device_id_type=MESH,
    )
    copy.start()
    return copy


def gather_kernel(mine, out, own_sem, y_sem, z_send, z_recv, c_send, c_recv):
    z, y, c = wide_place()
    right, left = wide_at(z + 1, y, c), wide_at(z - 1, y, c)
    across, partner = wide_at(z, 1 - y, c), wide_at(z, y, 1 - c)
    greet("wide", (right, left, across, partner))
    me = wide_at(z, y, c)
    rows = (y, 1 - y)
    ycopy = send("wide", across, mine, out.at[me], y_sem.at[0], y_sem.at[1])
    own = pltpu.make_async_copy(mine, out.at[me], own_sem)
    own.start()
    sent = [ycopy]
    cores = []

    def pass_on(src, slot):
        k = len(cores)
        cores.append(send("wide", partner, src, out.at[slot], c_send.at[k], c_recv.at[k]))

    last = {}
    for s in range(1, 10):
        for q in (0, 1):
            for d in (0, 1):
                steps = 8 - d
                if s > steps + 1:
                    continue
                origin = z - (s - 1) if d == 0 else z + (s - 1)
                slot = wide_at(origin, rows[q], c)
                src = out.at[slot]
                if s == 1:
                    if q == 0:
                        src = mine
                    elif d == 0:
                        ycopy.wait_recv()
                else:
                    last[d, q].wait_recv()
                if s <= steps:
                    k = (d * 2 + q) * 8 + s - 1
                    last[d, q] = send(
                        "wide",
                        right if d == 0 else left,
                        src,
                        out.at[slot],
                        z_send.at[k],
                        z_recv.at[k],
                    )
                    sent.append(last[d, q])
                if s > 1 or d == 0:
                    pass_on(src, slot)
    own.wait()
    for copy in cores:
        copy.wait_recv()
    for copy in sent + cores:
        copy.wait_send()


def gather_wide(mine):
    return pl.pallas_call(
        gather_kernel,
        out_shape=jax.ShapeDtypeStruct((4 * Z,) + mine.shape, mine.dtype),
        in_specs=[VMEM],
        out_specs=VMEM,
        scratch_shapes=[
            pltpu.SemaphoreType.DMA,
            pltpu.SemaphoreType.DMA((2,)),
            pltpu.SemaphoreType.DMA((32,)),
            pltpu.SemaphoreType.DMA((32,)),
            pltpu.SemaphoreType.DMA((32,)),
            pltpu.SemaphoreType.DMA((32,)),
        ],
        compiler_params=pltpu.CompilerParams(collective_id=0, has_side_effects=True),
        name="gather_wide",
    )(mine)


def forward_kernel(
    gu_index, gu_count, down_index, down_count, got, gate, up, down, part, wgu, wd, xs, dys
):
    wgu[...] = jnp.zeros_like(wgu)
    wd[...] = jnp.zeros_like(wd)
    for s in range(gate.shape[0]):

        @pl.when(s < gu_count[0])
        def _():
            at = gu_index[s]
            row = pl.multiple_of((at // 2) * B, B)
            col = pl.multiple_of((at % 2) * B, B)
            wgu[pl.ds(row, B), pl.ds(col, B)] = gate[s]
            wgu[pl.ds(row, B), pl.ds(2 * B + col, B)] = up[s]

        @pl.when(s < down_count[0])
        def _():
            at = down_index[s]
            row = pl.multiple_of((at // 8) * B, B)
            col = pl.multiple_of((at % 8) * B, B)
            wd[pl.ds(row, B), pl.ds(col, B)] = down[s]

    @pl.loop(0, 4)
    def _(i):
        rows = pl.ds(pl.multiple_of(i * B, B), B)
        some = pl.ds(i * (B // 8), B // 8)
        x = got[some, 0].astype(F32).reshape(B, -1).astype(BF16)
        dy = got[some, 1].astype(F32).reshape(B, -1).astype(BF16)
        xs[rows, :] = x
        dys[rows, :] = dy
        part[rows, : 4 * B] = jnp.dot(x, wgu[...], preferred_element_type=F32)
        part[rows, 4 * B :] = lax.dot_general(
            dy, wd[...], (((1,), (1,)), ((), ())), preferred_element_type=F32
        )


def forward(gu_index, gu_count, down_index, down_count, got, gate, up, down):
    return pl.pallas_call(
        forward_kernel,
        out_shape=(
            jax.ShapeDtypeStruct((512, 6 * B), F32),
            jax.ShapeDtypeStruct((1024, 4 * B), BF16),
            jax.ShapeDtypeStruct((2 * B, 1024), BF16),
            jax.ShapeDtypeStruct((512, 1024), BF16),
            jax.ShapeDtypeStruct((512, 1024), BF16),
        ),
        in_specs=[SMEM] * 4 + [VMEM] * 4,
        out_specs=(VMEM,) * 5,
        name="forward",
    )(gu_index, gu_count, down_index, down_count, got, gate, up, down)


ORDER = (4, 3, 5, 2, 6, 1, 7)


def narrow_kernel(part, out, got, s_send, s_recv, g_send, g_recv):
    n = lax.axis_index("narrow")
    peers = {k: (n + k) % N for k in ORDER}
    greet("narrow", tuple(peers.values()))
    sums = [
        send("narrow", peers[k], part.at[peers[k]], got.at[k], s_send.at[k], s_recv.at[k])
        for k in ORDER
    ]
    total = part[n]
    for copy, k in zip(sums, ORDER):
        copy.wait_recv()
        total = total + got[k]
    gate, up, d_hidden = total[:, : 2 * B], total[:, 2 * B : 4 * B], total[:, 4 * B :]
    sig = jax.nn.sigmoid(gate)
    out[n, :, : 2 * B] = (gate * sig * up).astype(BF16)
    out[n, :, 2 * B : 4 * B] = (d_hidden * up * sig * (1.0 + gate * (1.0 - sig))).astype(BF16)
    out[n, :, 4 * B :] = (d_hidden * gate * sig).astype(BF16)
    shares = [
        send("narrow", peers[k], out.at[n], out.at[n], g_send.at[k], g_recv.at[k]) for k in ORDER
    ]
    for copy in shares:
        copy.wait_recv()
    for copy in sums + shares:
        copy.wait_send()


def narrow_step(part):
    return pl.pallas_call(
        narrow_kernel,
        out_shape=jax.ShapeDtypeStruct(part.shape, BF16),
        in_specs=[VMEM],
        out_specs=VMEM,
        scratch_shapes=[pltpu.VMEM(part.shape, F32)] + [pltpu.SemaphoreType.DMA((N,))] * 4,
        compiler_params=pltpu.CompilerParams(collective_id=1, has_side_effects=True),
        name="narrow_step",
    )(part)


def backward_kernel(
    gu_index, gu_count, down_index, down_count, units, xs, dys, wgu, dx, gate_g, up_g, down_g, dgu, dd
):
    grads = units[:, 2 * B :]

    @pl.loop(0, 4)
    def _(i):
        rows = pl.ds(pl.multiple_of(i * B, B), B)
        dx[rows, :] = lax.dot_general(
            units[rows, 2 * B :], wgu[...], (((1,), (1,)), ((), ())), preferred_element_type=F32
        )

    @pl.loop(0, 4)
    def _(i):
        cols = pl.ds(pl.multiple_of(i * 2 * B, 2 * B), 2 * B)
        dgu[cols, :] = lax.dot_general(
            xs[:, cols], grads, (((0,), (0,)), ((), ())), preferred_element_type=F32
        ).astype(BF16)

    dd[...] = lax.dot_general(
        units[:, : 2 * B], dys[...], (((0,), (0,)), ((), ())), preferred_element_type=F32
    ).astype(BF16)
    for s in range(gate_g.shape[0]):
        alive = s < gu_count[0]

        @pl.when(alive)
        def _():
            at = gu_index[s]
            row = pl.multiple_of((at // 2) * B, B)
            col = pl.multiple_of((at % 2) * B, B)
            gate_g[s] = dgu[pl.ds(row, B), pl.ds(col, B)]
            up_g[s] = dgu[pl.ds(row, B), pl.ds(2 * B + col, B)]

        @pl.when(jnp.logical_not(alive))
        def _():
            gate_g[s] = jnp.zeros((B, B), BF16)
            up_g[s] = jnp.zeros((B, B), BF16)

        d_alive = s < down_count[0]

        @pl.when(d_alive)
        def _():
            at = down_index[s]
            row = pl.multiple_of((at // 8) * B, B)
            col = pl.multiple_of((at % 8) * B, B)
            down_g[s] = dd[pl.ds(row, B), pl.ds(col, B)]

        @pl.when(jnp.logical_not(d_alive))
        def _():
            down_g[s] = jnp.zeros((B, B), BF16)


def backward(gu_index, gu_count, down_index, down_count, units, xs, dys, wgu, slots):
    grad = jax.ShapeDtypeStruct((slots, B, B), BF16)
    return pl.pallas_call(
        backward_kernel,
        out_shape=(jax.ShapeDtypeStruct((512, 1024), F32), grad, grad, grad),
        in_specs=[SMEM] * 4 + [VMEM] * 4,
        out_specs=(VMEM,) * 4,
        scratch_shapes=[pltpu.VMEM((1024, 4 * B), BF16), pltpu.VMEM((2 * B, 1024), BF16)],
        name="backward",
    )(gu_index, gu_count, down_index, down_count, units, xs, dys, wgu)


def scatter_kernel(part, out, held, run, last, c_send, c_recv, z_send, z_recv, y_sem):
    z, y, c = wide_place()
    right, left = wide_at(z + 1, y, c), wide_at(z - 1, y, c)
    across, partner = wide_at(z, 1 - y, c), wide_at(z, y, 1 - c)
    greet("wide", (right, left, across, partner))
    rows = (1 - y, y)

    order = []
    for s in range(8):
        order.append(8 - s)
        if s < 7:
            order.append(s - 7)
    order.append(0)
    cores = {}
    for k, off in enumerate(order):
        t = (z + off + Z) % Z
        cores[off] = send(
            "wide", partner, part.at[t, :, 1 - c], held.at[t], c_send.at[k], c_recv.at[k]
        )
    sent = list(cores.values())

    def mine(off, q):
        t = (z + off + Z) % Z
        return part[t, rows[q], c] + held[t, rows[q]]

    prev = {}
    for s in range(8):
        for q in (0, 1):
            for d in (0, 1):
                if s >= 8 - d:
                    continue
                off = 8 - s if d == 0 else s - 7
                if q == 0:
                    cores[off].wait_recv()
                if s == 0:
                    run[d, q, s] = mine(off, q)
                else:
                    prev[d, q].wait_recv()
                    run[d, q, s] = run[d, q, s] + mine(off, q)
                k = (d * 2 + q) * 8 + s
                prev[d, q] = send(
                    "wide",
                    right if d == 0 else left,
                    run.at[d, q, s],
                    run.at[d, q, s + 1],
                    z_send.at[k],
                    z_recv.at[k],
                )
                sent.append(prev[d, q])
    cores[0].wait_recv()

    def total(q):
        prev[1, q].wait_recv()
        left_sum = run[1, q, 7] + mine(0, q)
        prev[0, q].wait_recv()
        return left_sum + run[0, q, 8]

    last[0] = total(0)
    ycopy = send("wide", across, last.at[0], last.at[1], y_sem.at[0], y_sem.at[1])
    own = total(1)
    ycopy.wait_recv()
    out[...] = (own + last[1]).astype(BF16)
    for copy in sent + [ycopy]:
        copy.wait_send()


def scatter_wide(part):
    width = part.shape[-1]
    return pl.pallas_call(
        scatter_kernel,
        out_shape=jax.ShapeDtypeStruct((8, width), BF16),
        in_specs=[VMEM],
        out_specs=VMEM,
        scratch_shapes=[
            pltpu.VMEM((Z, 2, 8, width), F32),
            pltpu.VMEM((2, 2, 9, 8, width), F32),
            pltpu.VMEM((2, 8, width), F32),
            pltpu.SemaphoreType.DMA((Z,)),
            pltpu.SemaphoreType.DMA((Z,)),
            pltpu.SemaphoreType.DMA((32,)),
            pltpu.SemaphoreType.DMA((32,)),
            pltpu.SemaphoreType.DMA((2,)),
        ],
        compiler_params=pltpu.CompilerParams(collective_id=2, has_side_effects=True),
        name="scatter_wide",
    )(part)


def on_device(
    tokens, cotangent, gate_vals, up_vals, gu_index, gu_count, down_vals, down_index, down_count
):
    tables = (gu_index[0, 0], gu_count[0], down_index[0, 0], down_count[0])
    got = gather_wide(jnp.stack([tokens, cotangent]))
    part, wgu, _, xs, dys = forward(*tables, got, gate_vals[0, 0], up_vals[0, 0], down_vals[0, 0])
    units = narrow_step(part.reshape(N, 64, 6 * B)).reshape(512, 6 * B)
    dx, gate_g, up_g, down_g = backward(*tables, units, xs, dys, wgu, gate_vals.shape[2])
    d_tokens = scatter_wide(dx.reshape(Z, 2, 2, 8, dx.shape[-1]))
    return (d_tokens, gate_g[None, None], up_g[None, None], down_g[None, None])


def solution(mesh):
    in_specs = (
        P("wide", "narrow"),
        P("wide", "narrow"),
        P("narrow", "wide", None, None, None),
        P("narrow", "wide", None, None, None),
        P("narrow", "wide", None),
        P("narrow", "wide"),
        P("wide", "narrow", None, None, None),
        P("wide", "narrow", None),
        P("wide", "narrow"),
    )
    out_specs = (
        P("wide", "narrow"),
        P("narrow", "wide", None, None, None),
        P("narrow", "wide", None, None, None),
        P("wide", "narrow", None, None, None),
    )
    return jax.shard_map(
        on_device, mesh=mesh, in_specs=in_specs, out_specs=out_specs, check_vma=False
    )
```

time: 693 us -> 138 us (0.20)
  waiting for transfers between devices: 510 us -> 0 us
  Pallas kernels: 0 us -> 133 us
  blocking collectives: 85.3 us -> 0 us
  local copies, waits for them, and re-layouts: 42.1 us -> 1.32 us
  matrix products: 32.8 us -> 0 us
  between operations: 15.3 us -> 1.95 us
    all_gather x2 -> x0, waiting for transfers between devices: 264 us -> none  [the longest x1 139 us: on_device(): dy_all = lax.all_gather(cotangent, 'wide', axis=0, tiled=True)]
    reduce_scatter x3 -> x0, waiting for transfers between devices: 245 us -> none  [the longest x1 178 us: on_device(): lax.psum_scatter(apply_blocks(grads_pair, paired, paired_cols, paired_row...]
    pallas_call x0 -> x5, Pallas kernels: none -> 133 us  [the longest x1 44.5 us: gather_wide(): pl.pallas_call(gather_kernel, out_shape=jax.ShapeDtypeStruct((4 * Z,) + m...]
    all_gather x3 -> x0, blocking collectives: 85.3 us -> none  [the longest x1 28.6 us: on_device(): lax.all_gather(d_up, 'narrow', axis=0, tiled=True)]
    dot_general x8 -> x0, matrix products: 32.8 us -> none  [the longest x3 13.6 us: apply_blocks(): jnp.einsum(form, picked, tile_values, preferred_element_type=jnp.float32)]
    transpose x3 -> x0, local copies, waits for them, and re-layouts: 16.7 us -> none  [apply_blocks(): jnp.einsum(form, picked, tile_values, preferred_element_type=jnp.float32)]
    gather x4 -> x0, local copies, waits for them, and re-layouts: 9.3 us -> none  [the longest x3 7.36 us: apply_blocks(): picked = jnp.take(pieces, source_blocks, axis=1)]
    unnamed x23 -> x1, local copies, waits for them, and re-layouts: 9.43 us -> 1.32 us
  transfers between devices with their start and end apart: 5 -> 0, of which waited for: 5 -> 0; matrix products, arithmetic and copies ran while one was open for 8% -> 0% of each run, Pallas kernels for 0% -> 0%
where the time goes in v1:
time: 138 us
  Pallas kernels  133 us (96%)
  between operations  1.95 us (1%)
    pallas_call x1, Pallas kernels, gather_wide(): pl.pallas_call(gather_kernel, out_shape=jax.ShapeDtypeStruct((4 * Z,) + m...  44.5 us
    pallas_call x1, Pallas kernels, narrow_step(): pl.pallas_call(narrow_kernel, out_shape=jax.ShapeDtypeStruct(part.shape,...  38.6 us
    pallas_call x1, Pallas kernels, scatter_wide(): pl.pallas_call(scatter_kernel, out_shape=jax.ShapeDtypeStruct((8, width),...  36.1 us
    pallas_call x1, Pallas kernels, backward(): pl.pallas_call(backward_kernel, out_shape=(jax.ShapeDtypeStruct((512, 102...  7.98 us
    pallas_call x1, Pallas kernels, forward(): pl.pallas_call(forward_kernel, out_shape=(jax.ShapeDtypeStruct((512, 6 *...  6 us

profile of v1, /device:TPU:6, one launch (start us, length us, event | category | flops | bytes accessed | tf_op | source)
XLA Modules:
  0.0 137.8 jit_solution(1357949611333248856)
XLA Ops:
  1.9 1.4 pad_maximum_fusion.mine
  3.3 44.5 %gather_wide.1.got = bf16[64,2,8,1024]{3,2,1,0:T(8,128)(2,1)} custom-call(bf16[2,8,1024]{2,1,0:T(8,128)(2,1)} %pad_maximum_fusion.mine), custom_call_target="tpu_custom_call" | custom-call | tf_op jit(solution)/shard_map/gather_wide/pallas_call | solution.py:103
  47.8 6.0 %forward.1 = (f32[512,768]{1,0:T(8,128)}, bf16[1024,512]{1,0:T(8,128)(2,1)}, bf16[256,1024]{1,0:T(8,128)(2,1)}, bf16[512,1024]{1,0:T(8,128)(2,1)}, bf16[512,1024]{1,0:T(8,128)(2,1)}) custom-call(s32[12]{0:T(128)} %bitcast.27, s32[1]{0:T(128)} %bitcast.15.gu_count, s32[12]{0:T(128)} %bitcast.29, s32[1]{0:T(128)} %bitcast.17.down_count, ...), custom_call_target="tpu_custom_call" | custom-call | tf_op jit(solution)/shard_map/forward/pallas_call | solution.py:158
  53.8 38.6 %narrow_step.1 = bf16[8,64,768]{2,1,0:T(8,128)(2,1)} custom-call(f32[8,64,768]{2,1,0:T(8,128)} %bitcast.21), custom_call_target="tpu_custom_call" | custom-call | tf_op jit(solution)/shard_map/narrow_step/pallas_call | solution.py:203
  92.4 8.0 %backward.1 = (f32[512,1024]{1,0:T(8,128)}, bf16[12,128,128]{2,1,0:T(8,128)(2,1)}, bf16[12,128,128]{2,1,0:T(8,128)(2,1)}, bf16[12,128,128]{2,1,0:T(8,128)(2,1)}) custom-call(s32[12]{0:T(128)} %bitcast.28, s32[1]{0:T(128)} %bitcast.16.gu_count, s32[12]{0:T(128)} %bitcast.30, s32[1]{0:T(128)} %bitcast.18.down_count, bf16[512,768]{1,0:T(8,128)(2,1)} %bitcast.19, ...), custom_call_target="tpu_custom_call" | custom-call | tf_op jit(solution)/shard_map/backward/pallas_call | solution.py:268
  100.4 36.1 %scatter_wide.1 = bf16[8,1024]{1,0:T(8,128)(2,1)} custom-call(f32[16,2,2,8,1024]{4,3,2,1,0:T(8,128)} %bitcast.20), custom_call_target="tpu_custom_call" | custom-call | tf_op jit(solution)/shard_map/scatter_wide/pallas_call | solution.py:346
  136.5 1.3 copy.16

commit v2 on v1

v2 whole, which is shorter than its diff:
```python
import jax
import jax.numpy as jnp
from jax import lax
from jax.experimental import pallas as pl
from jax.experimental.pallas import tpu as pltpu
from jax.sharding import PartitionSpec as P

MESH = pl.DeviceIdType.MESH
VMEM = pl.BlockSpec(memory_space=pltpu.VMEM)
SMEM = pl.BlockSpec(memory_space=pltpu.SMEM)
F32 = jnp.float32
BF16 = jnp.bfloat16

Z = 16
N = 8
B = 128


def wide_place():
    w = lax.axis_index("wide")
    return w // 4, (w // 2) % 2, w % 2


def wide_at(z, y, c):
    return ((z + Z) % Z * 2 + y) * 2 + c


def greet(peers):
    barrier = pltpu.get_barrier_semaphore()
    for axis, peer in peers:
        pl.semaphore_signal(barrier, inc=1, device_id={axis: peer}, device_id_type=MESH)
    pl.semaphore_wait(barrier, len(peers))


def send(axis, peer, src, dst, send_sem, recv_sem):
    copy = pltpu.make_async_remote_copy(
        src_ref=src,
        dst_ref=dst,
        send_sem=send_sem,
        recv_sem=recv_sem,
        device_id={axis: peer},
        device_id_type=MESH,
    )
    copy.start()
    return copy


def build_kernel(gu_index, gu_count, down_index, down_count, gate, up, down, wgu, wd):
    wgu[...] = jnp.zeros_like(wgu)
    wd[...] = jnp.zeros_like(wd)
    for s in range(gate.shape[0]):

        @pl.when(s < gu_count[0])
        def _():
            at = gu_index[s]
            row = pl.multiple_of((at // 2) * B, B)
            col = pl.multiple_of((at % 2) * B, B)
            wgu[pl.ds(row, B), pl.ds(col, B)] = gate[s]
            wgu[pl.ds(row, B), pl.ds(2 * B + col, B)] = up[s]

        @pl.when(s < down_count[0])
        def _():
            at = down_index[s]
            row = pl.multiple_of((at // 8) * B, B)
            col = pl.multiple_of((at % 8) * B, B)
            wd[pl.ds(row, B), pl.ds(col, B)] = down[s]


def build(tables, gate, up, down):
    return pl.pallas_call(
        build_kernel,
        out_shape=(
            jax.ShapeDtypeStruct((8 * B, 4 * B), BF16),
            jax.ShapeDtypeStruct((2 * B, 8 * B), BF16),
        ),
        in_specs=[SMEM] * 4 + [VMEM] * 3,
        out_specs=(VMEM,) * 2,
        name="build",
    )(*tables, gate, up, down)


ORDER = (4, 3, 5, 2, 6, 1, 7)


def front_kernel(
    mine,
    wgu,
    wd,
    units,
    xs,
    dys,
    got,
    part,
    sums,
    own_sem,
    y_sem,
    z_send,
    z_recv,
    c_send,
    c_recv,
    s_send,
    s_recv,
    g_send,
    g_recv,
):
    z, y, c = wide_place()
    n = lax.axis_index("narrow")
    right, left = wide_at(z + 1, y, c), wide_at(z - 1, y, c)
    across, partner = wide_at(z, 1 - y, c), wide_at(z, y, 1 - c)
    peers = {k: (n + k) % N for k in ORDER}
    greet([("wide", w) for w in (right, left, across, partner)] + [("narrow", p) for p in peers.values()])
    me = wide_at(z, y, c)
    rows = (y, 1 - y)
    ycopy = send("wide", across, mine, got.at[me], y_sem.at[0], y_sem.at[1])
    own = pltpu.make_async_copy(mine, got.at[me], own_sem)
    own.start()
    sent = [ycopy]
    cores = {}
    last = {}
    reduces = {}
    shares = []

    def ring(s):
        for q in (0, 1):
            for d in (0, 1):
                steps = 8 - d
                if s > steps + 1:
                    continue
                off = 1 - s if d == 0 else s - 1
                slot = wide_at(z + off, rows[q], c)
                src = got.at[slot]
                if s == 1:
                    if q == 0:
                        src = mine
                    elif d == 0:
                        ycopy.wait_recv()
                else:
                    last[d, q].wait_recv()
                if s <= steps:
                    k = (d * 2 + q) * 8 + s - 1
                    last[d, q] = send(
                        "wide",
                        right if d == 0 else left,
                        src,
                        got.at[slot],
                        z_send.at[k],
                        z_recv.at[k],
                    )
                    sent.append(last[d, q])
                if s > 1 or d == 0:
                    k = len(cores)
                    cores[off, q] = send(
                        "wide", partner, src, got.at[slot], c_send.at[k], c_recv.at[k]
                    )

    def chunk(k):
        offs = (-k, k) if k < 8 else (0, -8)
        for off in offs:
            for q in (0, 1):
                cores[off, q].wait_recv()
        slots = [wide_at(z + off, yy, cc) for off in offs for yy in (0, 1) for cc in (0, 1)]

        def rows_of(which):
            return jnp.concatenate([got[slot, which].astype(F32) for slot in slots], axis=0).astype(BF16)

        x = rows_of(0)
        xs[k - 1] = x
        gu = jnp.dot(x, wgu[...], preferred_element_type=F32)
        part[k - 1, :, :, : 4 * B] = gu.reshape(8, 8, 4 * B)
        dy = rows_of(1)
        dys[k - 1] = dy
        dh = lax.dot_general(dy, wd[...], (((1,), (1,)), ((), ())), preferred_element_type=F32)
        part[k - 1, :, :, 4 * B :] = dh.reshape(8, 8, 2 * B)
        for j in ORDER:
            reduces[k, j] = send(
                "narrow",
                peers[j],
                part.at[k - 1, peers[j]],
                sums.at[k - 1, j],
                s_send.at[k - 1, j],
                s_recv.at[k - 1, j],
            )

    def finish(k):
        total = part[k - 1, n]
        for j in ORDER:
            reduces[k, j].wait_recv()
            total = total + sums[k - 1, j]
        gate, up, d_hidden = total[:, : 2 * B], total[:, 2 * B : 4 * B], total[:, 4 * B :]
        sig = jax.nn.sigmoid(gate)
        units[k - 1, n, :, : 2 * B] = (gate * sig * up).astype(BF16)
        units[k - 1, n, :, 2 * B : 4 * B] = (
            d_hidden * up * sig * (1.0 + gate * (1.0 - sig))
        ).astype(BF16)
        units[k - 1, n, :, 4 * B :] = (d_hidden * gate * sig).astype(BF16)
        for j in ORDER:
            shares.append(
                send(
                    "narrow",
                    peers[j],
                    units.at[k - 1, n],
                    units.at[k - 1, n],
                    g_send.at[k - 1, j],
                    g_recv.at[k - 1, j],
                )
            )

    ring(1)
    own.wait()
    for s in range(2, 10):
        ring(s)
        chunk(s - 1)
        if s > 2:
            finish(s - 2)
    finish(8)
    for copy in shares:
        copy.wait_recv()
    for copy in sent + list(cores.values()) + list(reduces.values()) + shares:
        copy.wait_send()


def front(mine, wgu, wd):
    width = mine.shape[-1]
    sem = pltpu.SemaphoreType.DMA
    return pl.pallas_call(
        front_kernel,
        out_shape=(
            jax.ShapeDtypeStruct((8, N, 8, 6 * B), BF16),
            jax.ShapeDtypeStruct((8, 64, width), BF16),
            jax.ShapeDtypeStruct((8, 64, width), BF16),
        ),
        in_specs=[VMEM] * 3,
        out_specs=(VMEM,) * 3,
        scratch_shapes=[
            pltpu.VMEM((4 * Z,) + mine.shape, BF16),
            pltpu.VMEM((8, N, 8, 6 * B), F32),
            pltpu.VMEM((8, N, 8, 6 * B), F32),
            sem,
            sem((2,)),
            sem((32,)),
            sem((32,)),
            sem((32,)),
            sem((32,)),
            sem((8, N)),
            sem((8, N)),
            sem((8, N)),
            sem((8, N)),
        ],
        compiler_params=pltpu.CompilerParams(collective_id=0, has_side_effects=True),
        name="front",
    )(mine, wgu, wd)


def grads_kernel(
    gu_index, gu_count, down_index, down_count, units, xs, dys, gate_g, up_g, down_g, dgu, dd
):
    grads = units[:, 2 * B :]

    @pl.loop(0, 4)
    def _(i):
        cols = pl.ds(pl.multiple_of(i * 2 * B, 2 * B), 2 * B)
        dgu[cols, :] = lax.dot_general(
            xs[:, cols], grads, (((0,), (0,)), ((), ())), preferred_element_type=F32
        ).astype(BF16)

    dd[...] = lax.dot_general(
        units[:, : 2 * B], dys[...], (((0,), (0,)), ((), ())), preferred_element_type=F32
    ).astype(BF16)
    for s in range(gate_g.shape[0]):
        alive = s < gu_count[0]

        @pl.when(alive)
        def _():
            at = gu_index[s]
            row = pl.multiple_of((at // 2) * B, B)
            col = pl.multiple_of((at % 2) * B, B)
            gate_g[s] = dgu[pl.ds(row, B), pl.ds(col, B)]
            up_g[s] = dgu[pl.ds(row, B), pl.ds(2 * B + col, B)]

        @pl.when(jnp.logical_not(alive))
        def _():
            gate_g[s] = jnp.zeros((B, B), BF16)
            up_g[s] = jnp.zeros((B, B), BF16)

        d_alive = s < down_count[0]

        @pl.when(d_alive)
        def _():
            at = down_index[s]
            row = pl.multiple_of((at // 8) * B, B)
            col = pl.multiple_of((at % 8) * B, B)
            down_g[s] = dd[pl.ds(row, B), pl.ds(col, B)]

        @pl.when(jnp.logical_not(d_alive))
        def _():
            down_g[s] = jnp.zeros((B, B), BF16)


def block_grads(tables, units, xs, dys, slots):
    grad = jax.ShapeDtypeStruct((slots, B, B), BF16)
    return pl.pallas_call(
        grads_kernel,
        out_shape=(grad, grad, grad),
        in_specs=[SMEM] * 4 + [VMEM] * 3,
        out_specs=(VMEM,) * 3,
        scratch_shapes=[pltpu.VMEM((1024, 4 * B), BF16), pltpu.VMEM((2 * B, 1024), BF16)],
        name="block_grads",
    )(*tables, units, xs, dys)


def chunk_of(off):
    if off in (0, 8):
        return 7, (off == 8) * 1
    return abs(off) - 1, (off > 0) * 1


def scatter_kernel(units, wgu, out, part, held, run, last, c_send, c_recv, z_send, z_recv, y_sem):
    z, y, c = wide_place()
    right, left = wide_at(z + 1, y, c), wide_at(z - 1, y, c)
    across, partner = wide_at(z, 1 - y, c), wide_at(z, y, 1 - c)
    greet([("wide", w) for w in (right, left, across, partner)])
    rows = (1 - y, y)
    cores = {}

    def terms(s):
        offs = (8 - s, s - 7)
        places = [chunk_of(off) for off in offs]
        picked = jnp.concatenate(
            [units[k, 4 * 8 * j : 4 * 8 * (j + 1), 2 * B :] for k, j in places], axis=0
        )
        dx = lax.dot_general(
            picked, wgu[...], (((1,), (1,)), ((), ())), preferred_element_type=F32
        ).reshape(2, 2, 2, 8, -1)
        for i, (k, j) in enumerate(places):
            part[k, j] = dx[i]
            a = 2 * s + i
            cores[offs[i]] = send(
                "wide", partner, part.at[k, j, :, 1 - c], held.at[k, j], c_send.at[a], c_recv.at[a]
            )

    def mine(off, q):
        k, j = chunk_of(off)
        return part[k, j, rows[q], c] + held[k, j, rows[q]]

    prev = {}
    sent = []
    terms(0)
    terms(1)
    for s in range(8):
        for q in (0, 1):
            for d in (0, 1):
                if s >= 8 - d:
                    continue
                off = 8 - s if d == 0 else s - 7
                if q == 0:
                    cores[off].wait_recv()
                if s == 0:
                    run[d, q, s] = mine(off, q)
                else:
                    prev[d, q].wait_recv()
                    run[d, q, s] = run[d, q, s] + mine(off, q)
                k = (d * 2 + q) * 8 + s
                prev[d, q] = send(
                    "wide",
                    right if d == 0 else left,
                    run.at[d, q, s],
                    run.at[d, q, s + 1],
                    z_send.at[k],
                    z_recv.at[k],
                )
                sent.append(prev[d, q])
        if s + 2 < 8:
            terms(s + 2)
    cores[0].wait_recv()

    def total(q):
        prev[1, q].wait_recv()
        left_sum = run[1, q, 7] + mine(0, q)
        prev[0, q].wait_recv()
        return left_sum + run[0, q, 8]

    last[0] = total(0)
    ycopy = send("wide", across, last.at[0], last.at[1], y_sem.at[0], y_sem.at[1])
    own = total(1)
    ycopy.wait_recv()
    out[...] = (own + last[1]).astype(BF16)
    for copy in sent + list(cores.values()) + [ycopy]:
        copy.wait_send()


def scatter_wide(units, wgu):
    width = wgu.shape[0]
    sem = pltpu.SemaphoreType.DMA
    return pl.pallas_call(
        scatter_kernel,
        out_shape=jax.ShapeDtypeStruct((8, width), BF16),
        in_specs=[VMEM] * 2,
        out_specs=VMEM,
        scratch_shapes=[
            pltpu.VMEM((8, 2, 2, 2, 8, width), F32),
            pltpu.VMEM((8, 2, 2, 8, width), F32),
            pltpu.VMEM((2, 2, 9, 8, width), F32),
            pltpu.VMEM((2, 8, width), F32),
            sem((Z,)),
            sem((Z,)),
            sem((32,)),
            sem((32,)),
            sem((2,)),
        ],
        compiler_params=pltpu.CompilerParams(collective_id=2, has_side_effects=True),
        name="scatter_wide",
    )(units, wgu)


def on_device(
    tokens, cotangent, gate_vals, up_vals, gu_index, gu_count, down_vals, down_index, down_count
):
    tables = (gu_index[0, 0], gu_count[0], down_index[0, 0], down_count[0])
    wgu, wd = build(tables, gate_vals[0, 0], up_vals[0, 0], down_vals[0, 0])
    units, xs, dys = front(jnp.stack([tokens, cotangent]), wgu, wd)
    d_tokens = scatter_wide(units.reshape(8, 64, -1), wgu)
    gate_g, up_g, down_g = block_grads(
        tables, *(v.reshape(512, -1) for v in (units, xs, dys)), gate_vals.shape[2]
    )
    return (d_tokens, gate_g[None, None], up_g[None, None], down_g[None, None])


def solution(mesh):
    in_specs = (
        P("wide", "narrow"),
        P("wide", "narrow"),
        P("narrow", "wide", None, None, None),
        P("narrow", "wide", None, None, None),
        P("narrow", "wide", None),
        P("narrow", "wide"),
        P("wide", "narrow", None, None, None),
        P("wide", "narrow", None),
        P("wide", "narrow"),
    )
    out_specs = (
        P("wide", "narrow"),
        P("narrow", "wide", None, None, None),
        P("narrow", "wide", None, None, None),
        P("wide", "narrow", None, None, None),
    )
    return jax.shard_map(
        on_device, mesh=mesh, in_specs=in_specs, out_specs=out_specs, check_vma=False
    )
```

time: 138 us -> 110 us (0.80)
  Pallas kernels: 133 us -> 105 us
    pallas_call x4 -> x3, Pallas kernels: 97.1 us -> 68.4 us  [the longest x1 60.5 us: front(): pl.pallas_call(front_kernel, out_shape=(jax.ShapeDtypeStruct((8, N, 8, 6...]
where the time goes in v2:
time: 110 us; the launch traced here: 109 us
  Pallas kernels  105 us (95%)
  between operations  1.98 us (2%)
  other arithmetic  1.34 us (1%)
    pallas_call x1, Pallas kernels, front(): pl.pallas_call(front_kernel, out_shape=(jax.ShapeDtypeStruct((8, N, 8, 6...  60.5 us
    pallas_call x1, Pallas kernels, scatter_wide(): pl.pallas_call(scatter_kernel, out_shape=jax.ShapeDtypeStruct((8, width),...  36.3 us
    pallas_call x1, Pallas kernels, block_grads(): pl.pallas_call(grads_kernel, out_shape=(grad, grad, grad), in_specs=[SMEM...  5.13 us
    pallas_call x1, Pallas kernels, build(): pl.pallas_call(build_kernel, out_shape=(jax.ShapeDtypeStruct((8 * B, 4 *...  2.81 us

profile of v2, /device:TPU:6, one launch (start us, length us, event | category | flops | bytes accessed | tf_op | source)
XLA Modules:
  0.0 108.6 jit_solution(11100266144622360871)
XLA Ops:
  0.6 0.0 copy-start.1
  1.9 0.0 copy-done.1
  2.0 1.3 %pad_maximum_fusion.mine = bf16[2,8,1024]{2,1,0:T(8,128)(2,1)} fusion(bf16[1,8,1024]{2,1,0:T(8,128)(2,1)S(1)} %bitcast.27, bf16[1,8,1024]{2,1,0:T(8,128)(2,1)} %bitcast.28), kind=kLoop, calls=%fused_computation | loop fusion | flops 16384 | bytes 65536 | tf_op jit(solution)/shard_map/stack | solution.py:420
  3.3 2.8 %build.1 = (bf16[1024,512]{1,0:T(8,128)(2,1)}, bf16[256,1024]{1,0:T(8,128)(2,1)}) custom-call(s32[12]{0:T(128)} %bitcast.29, s32[1]{0:T(128)} %bitcast.16.gu_count, s32[12]{0:T(128)} %bitcast.31, s32[1]{0:T(128)} %bitcast.18.down_count, bf16[12,128,128]{2,1,0:T(8,128)(2,1)} %bitcast.24, bf16[12,128,128]{2,1,0:T(8,128)(2,1)} %bitcast.25, ...), custom_call_target="tpu_custom_call" | custom-call | tf_op jit(solution)/shard_map/build/pallas_call | solution.py:70
  6.1 60.5 %front.1 = (bf16[8,8,8,768]{3,2,1,0:T(8,128)(2,1)}, bf16[8,64,1024]{2,1,0:T(8,128)(2,1)}, bf16[8,64,1024]{2,1,0:T(8,128)(2,1)}) custom-call(bf16[2,8,1024]{2,1,0:T(8,128)(2,1)} %pad_maximum_fusion.mine, bf16[1024,512]{1,0:T(8,128)(2,1)} %get-tuple-element.12.wgu, bf16[256,1024]{1,0:T(8,128)(2,1)} %get-tuple-element.13.wd), custom_call_target="tpu_custom_call" | custom-call | tf_op jit(solution)/shard_map/front/pallas_call | solution.py:225
  66.6 36.3 %scatter_wide.1 = bf16[8,1024]{1,0:T(8,128)(2,1)} custom-call(bf16[8,64,768]{2,1,0:T(8,128)(2,1)} %bitcast.20, bf16[1024,512]{1,0:T(8,128)(2,1)} %get-tuple-element.12.wgu), custom_call_target="tpu_custom_call" | custom-call | tf_op jit(solution)/shard_map/scatter_wide/pallas_call | solution.py:394
  102.9 0.0 copy-start
  102.9 5.1 %block_grads.1 = (bf16[12,128,128]{2,1,0:T(8,128)(2,1)}, bf16[12,128,128]{2,1,0:T(8,128)(2,1)}, bf16[12,128,128]{2,1,0:T(8,128)(2,1)}) custom-call(s32[12]{0:T(128)} %bitcast.30, s32[1]{0:T(128)} %bitcast.17.gu_count, s32[12]{0:T(128)} %bitcast.32, s32[1]{0:T(128)} %bitcast.19.down_count, bf16[512,768]{1,0:T(8,128)(2,1)} %bitcast.21, ...), custom_call_target="tpu_custom_call" | custom-call | tf_op jit(solution)/shard_map/block_grads/pallas_call | solution.py:301
  108.0 0.0 copy-done
  108.0 0.6 copy.16
Async XLA Ops:
  0.6 1.3 %copy-start.1 = (bf16[8,1024]{1,0:T(8,128)(2,1)S(1)}, bf16[8,1024]{1,0:T(8,128)(2,1)}, u32[]{:S(2)}) copy-start(bf16[8,1024]{1,0:T(8,128)(2,1)} %param.10) | copy-start | bytes 49156
  102.9 5.1 %copy-start = (bf16[8,1024]{1,0:T(8,128)(2,1)S(1)}, bf16[8,1024]{1,0:T(8,128)(2,1)}, u32[]{:S(2)}) copy-start(bf16[8,1024]{1,0:T(8,128)(2,1)} %scatter_wide.1) | copy-start | bytes 49156

commit v3 on v2

v3 whole, which is shorter than its diff:
```python
import jax
import jax.numpy as jnp
from jax import lax
from jax.experimental import pallas as pl
from jax.experimental.pallas import tpu as pltpu
from jax.sharding import PartitionSpec as P

MESH = pl.DeviceIdType.MESH
VMEM = pl.BlockSpec(memory_space=pltpu.VMEM)
SMEM = pl.BlockSpec(memory_space=pltpu.SMEM)
F32 = jnp.float32
BF16 = jnp.bfloat16

Z = 16
N = 8
B = 128


def wide_place():
    w = lax.axis_index("wide")
    return w // 4, (w // 2) % 2, w % 2


def wide_at(z, y, c):
    return ((z + Z) % Z * 2 + y) * 2 + c


def greet(peers):
    barrier = pltpu.get_barrier_semaphore()
    for axis, peer in peers:
        pl.semaphore_signal(barrier, inc=1, device_id={axis: peer}, device_id_type=MESH)
    pl.semaphore_wait(barrier, len(peers))


def send(axis, peer, src, dst, send_sem, recv_sem):
    copy = pltpu.make_async_remote_copy(
        src_ref=src,
        dst_ref=dst,
        send_sem=send_sem,
        recv_sem=recv_sem,
        device_id={axis: peer},
        device_id_type=MESH,
    )
    copy.start()
    return copy


def tables_kernel(gu_index, gu_count, down_index, down_count, out):
    for base, index, count in ((0, gu_index, gu_count), (4, down_index, down_count)):
        live = count[0, 0]
        for block in range(16):
            out[base + 2, block] = 0
            out[base + 3, block] = 0
        for s in range(index.shape[-1]):
            at = index[0, 0, s]
            out[base, s] = at
            out[base + 1, s] = jnp.where(s < live, 1, 0)

            @pl.when(s < live)
            def _():
                out[base + 2, at] = s
                out[base + 3, at] = 1


def tables_of(*args):
    return pl.pallas_call(
        tables_kernel,
        out_shape=jax.ShapeDtypeStruct((8, 16), jnp.int32),
        in_specs=[SMEM] * 4,
        out_specs=SMEM,
        name="tables",
    )(*args)


def only_if(flag, value):
    return jnp.where(jnp.full(value.shape, flag) > 0, value.astype(F32), 0.0).astype(BF16)


ORDER = (4, 3, 5, 2, 6, 1, 7)


def front_kernel(
    tables,
    tokens,
    cotangent,
    gate,
    up,
    down,
    units,
    wgu,
    xs,
    dys,
    wd,
    got,
    part,
    sums,
    own_sem,
    y_sem,
    z_send,
    z_recv,
    c_send,
    c_recv,
    s_send,
    s_recv,
    g_send,
    g_recv,
):
    z, y, c = wide_place()
    n = lax.axis_index("narrow")
    right, left = wide_at(z + 1, y, c), wide_at(z - 1, y, c)
    across, partner = wide_at(z, 1 - y, c), wide_at(z, y, 1 - c)
    peers = {k: (n + k) % N for k in ORDER}
    me = wide_at(z, y, c)
    owns = [
        pltpu.make_async_copy(ref, got.at[me, i], own_sem.at[i])
        for i, ref in enumerate((tokens, cotangent))
    ]
    for copy in owns:
        copy.start()
    greet([("wide", w) for w in (right, left, across, partner)] + [("narrow", p) for p in peers.values()])
    for copy in owns:
        copy.wait()
    mine = got.at[me]
    rows = (y, 1 - y)
    ycopy = send("wide", across, mine, got.at[me], y_sem.at[0], y_sem.at[1])
    sent = [ycopy]
    cores = {}
    last = {}
    reduces = {}
    shares = []

    def ring(s, q):
        for d in (0, 1):
            steps = 8 - d
            if s > steps + 1:
                continue
            off = 1 - s if d == 0 else s - 1
            slot = wide_at(z + off, rows[q], c)
            src = got.at[slot]
            if s > 1:
                last[d, q].wait_recv()
            elif q == 1 and d == 0:
                ycopy.wait_recv()
            if s <= steps:
                k = (d * 2 + q) * 8 + s - 1
                last[d, q] = send(
                    "wide", right if d == 0 else left, src, src, z_send.at[k], z_recv.at[k]
                )
                sent.append(last[d, q])
            if s > 1 or d == 0:
                k = len(cores)
                cores[off, q] = send("wide", partner, src, src, c_send.at[k], c_recv.at[k])

    def chunk(k):
        offs = (-k, k) if k < 8 else (0, -8)
        for off in offs:
            for q in (0, 1):
                cores[off, q].wait_recv()
        slots = [wide_at(z + off, yy, cc) for off in offs for yy in (0, 1) for cc in (0, 1)]

        def rows_of(which):
            return jnp.concatenate([got[slot, which].astype(F32) for slot in slots], axis=0).astype(BF16)

        x = rows_of(0)
        xs[k - 1] = x
        gu = jnp.dot(x, wgu[...], preferred_element_type=F32)
        part[k - 1, :, :, : 4 * B] = gu.reshape(8, 8, 4 * B)
        dy = rows_of(1)
        dys[k - 1] = dy
        dh = lax.dot_general(dy, wd[...], (((1,), (1,)), ((), ())), preferred_element_type=F32)
        part[k - 1, :, :, 4 * B :] = dh.reshape(8, 8, 2 * B)
        for j in ORDER:
            reduces[k, j] = send(
                "narrow",
                peers[j],
                part.at[k - 1, peers[j]],
                sums.at[k - 1, j],
                s_send.at[k - 1, j],
                s_recv.at[k - 1, j],
            )

    def finish(k):
        total = part[k - 1, n]
        for j in ORDER:
            reduces[k, j].wait_recv()
            total = total + sums[k - 1, j]
        gate, up, d_hidden = total[:, : 2 * B], total[:, 2 * B : 4 * B], total[:, 4 * B :]
        sig = jax.nn.sigmoid(gate)
        units[k - 1, n, :, : 2 * B] = (gate * sig * up).astype(BF16)
        units[k - 1, n, :, 2 * B : 4 * B] = (
            d_hidden * up * sig * (1.0 + gate * (1.0 - sig))
        ).astype(BF16)
        units[k - 1, n, :, 4 * B :] = (d_hidden * gate * sig).astype(BF16)
        for j in ORDER:
            shares.append(
                send(
                    "narrow",
                    peers[j],
                    units.at[k - 1, n],
                    units.at[k - 1, n],
                    g_send.at[k - 1, j],
                    g_recv.at[k - 1, j],
                )
            )

    def place(table, sources, target, width):
        for block in range(16):
            row, col = block // width * B, block % width * B
            slot, flag = tables[table + 2, block], tables[table + 3, block]
            for i, source in enumerate(sources):
                at = 2 * B * i + col
                target[row : row + B, at : at + B] = only_if(flag, source[slot])

    for i in range(1, 12):
        if i <= 9:
            ring(i, 0)
        if i == 1:
            place(0, (gate, up), wgu, 2)
            place(4, (down,), wd, 8)
        elif i <= 10:
            ring(i - 1, 1)
        if i > 3:
            chunk(i - 3)
        if i > 4:
            finish(i - 4)
    finish(8)
    for copy in shares:
        copy.wait_recv()
    for copy in sent + list(cores.values()) + list(reduces.values()) + shares:
        copy.wait_send()


def front(tables, tokens, cotangent, gate, up, down):
    width = tokens.shape[-1]
    sem = pltpu.SemaphoreType.DMA
    return pl.pallas_call(
        front_kernel,
        out_shape=(
            jax.ShapeDtypeStruct((8, N, 8, 6 * B), BF16),
            jax.ShapeDtypeStruct((8 * B, 4 * B), BF16),
            jax.ShapeDtypeStruct((8, 64, width), BF16),
            jax.ShapeDtypeStruct((8, 64, width), BF16),
        ),
        in_specs=[SMEM] + [VMEM] * 5,
        out_specs=(VMEM,) * 4,
        scratch_shapes=[
            pltpu.VMEM((2 * B, 8 * B), BF16),
            pltpu.VMEM((4 * Z, 2, 8, width), BF16),
            pltpu.VMEM((8, N, 8, 6 * B), F32),
            pltpu.VMEM((8, N, 8, 6 * B), F32),
            sem((2,)),
            sem((2,)),
            sem((32,)),
            sem((32,)),
            sem((32,)),
            sem((32,)),
            sem((8, N)),
            sem((8, N)),
            sem((8, N)),
            sem((8, N)),
        ],
        compiler_params=pltpu.CompilerParams(collective_id=0, has_side_effects=True),
        name="front",
    )(tables, tokens, cotangent, gate, up, down)


def chunk_of(off):
    if off in (0, 8):
        return 7, (off == 8) * 1
    return abs(off) - 1, (off > 0) * 1


def back_kernel(
    tables,
    units,
    wgu,
    xs,
    dys,
    out,
    gate_g,
    up_g,
    down_g,
    dgu,
    dd,
    part,
    held,
    run,
    last,
    c_send,
    c_recv,
    z_send,
    z_recv,
    y_sem,
):
    z, y, c = wide_place()
    right, left = wide_at(z + 1, y, c), wide_at(z - 1, y, c)
    across, partner = wide_at(z, 1 - y, c), wide_at(z, y, 1 - c)
    greet([("wide", w) for w in (right, left, across, partner)])
    rows = (1 - y, y)
    cores = {}

    def terms(s):
        offs = (8 - s, s - 7)
        places = [chunk_of(off) for off in offs]
        picked = jnp.concatenate(
            [units[64 * k + 32 * j : 64 * k + 32 * (j + 1), 2 * B :] for k, j in places], axis=0
        )
        dx = lax.dot_general(
            picked, wgu[...], (((1,), (1,)), ((), ())), preferred_element_type=F32
        ).reshape(2, 2, 2, 8, -1)
        for i, (k, j) in enumerate(places):
            part[k, j] = dx[i]
            a = 2 * s + i
            cores[offs[i]] = send(
                "wide", partner, part.at[k, j, :, 1 - c], held.at[k, j], c_send.at[a], c_recv.at[a]
            )

    def mine(off, q):
        k, j = chunk_of(off)
        return part[k, j, rows[q], c] + held[k, j, rows[q]]

    def across_tokens(a, b):
        return lax.dot_general(
            a, b, (((0,), (0,)), ((), ())), preferred_element_type=F32
        ).astype(BF16)

    def gradients(s):
        if s < 4:
            dense = across_tokens(xs[:, 2 * B * s : 2 * B * (s + 1)], units[:, 2 * B :])
            for row in (0, 1):
                for i in (0, 1):
                    for col in (0, 1):
                        at = B * (2 * i + col)
                        dgu[i, 2 * (2 * s + row) + col] = dense[row * B : (row + 1) * B, at : at + B]
        elif s < 6:
            half = s - 4
            dense = across_tokens(units[:, : 2 * B], dys[:, 4 * B * half : 4 * B * (half + 1)])
            for row in (0, 1):
                for col in range(4):
                    dd[8 * row + 4 * half + col] = dense[row * B : (row + 1) * B, col * B : (col + 1) * B]
        elif s == 6:
            for k in range(gate_g.shape[0]):
                gate_g[k] = only_if(tables[1, k], dgu[0, tables[0, k]])
                up_g[k] = only_if(tables[1, k], dgu[1, tables[0, k]])
        else:
            for k in range(down_g.shape[0]):
                down_g[k] = only_if(tables[5, k], dd[tables[4, k]])

    prev = {}
    sent = []
    terms(0)
    terms(1)

    def step(s, q):
        for d in (0, 1):
            if s >= 8 - d:
                continue
            off = 8 - s if d == 0 else s - 7
            if q == 0:
                cores[off].wait_recv()
            if s == 0:
                run[d, q, s] = mine(off, q)
            else:
                prev[d, q].wait_recv()
                run[d, q, s] = run[d, q, s] + mine(off, q)
            k = (d * 2 + q) * 8 + s
            prev[d, q] = send(
                "wide",
                right if d == 0 else left,
                run.at[d, q, s],
                run.at[d, q, s + 1],
                z_send.at[k],
                z_recv.at[k],
            )
            sent.append(prev[d, q])

    for i in range(9):
        if i < 8:
            step(i, 0)
        if i > 0:
            step(i - 1, 1)
        if i + 2 < 8:
            terms(i + 2)
        if i < 8:
            gradients(i)
    cores[0].wait_recv()

    def total(q):
        prev[1, q].wait_recv()
        left_sum = run[1, q, 7] + mine(0, q)
        prev[0, q].wait_recv()
        return left_sum + run[0, q, 8]

    last[0] = total(0)
    ycopy = send("wide", across, last.at[0], last.at[1], y_sem.at[0], y_sem.at[1])
    own = total(1)
    ycopy.wait_recv()
    out[...] = (own + last[1]).astype(BF16)
    for copy in sent + list(cores.values()) + [ycopy]:
        copy.wait_send()


def back(tables, units, wgu, xs, dys, slots):
    width = wgu.shape[0]
    sem = pltpu.SemaphoreType.DMA
    grad = jax.ShapeDtypeStruct((slots, B, B), BF16)
    return pl.pallas_call(
        back_kernel,
        out_shape=(jax.ShapeDtypeStruct((8, width), BF16), grad, grad, grad),
        in_specs=[SMEM] + [VMEM] * 4,
        out_specs=(VMEM,) * 4,
        scratch_shapes=[
            pltpu.VMEM((2, 16, B, B), BF16),
            pltpu.VMEM((16, B, B), BF16),
            pltpu.VMEM((8, 2, 2, 2, 8, width), F32),
            pltpu.VMEM((8, 2, 2, 8, width), F32),
            pltpu.VMEM((2, 2, 9, 8, width), F32),
            pltpu.VMEM((2, 8, width), F32),
            sem((Z,)),
            sem((Z,)),
            sem((32,)),
            sem((32,)),
            sem((2,)),
        ],
        compiler_params=pltpu.CompilerParams(collective_id=2, has_side_effects=True),
        name="back",
    )(tables, units, wgu, xs, dys)


def on_device(
    tokens, cotangent, gate_vals, up_vals, gu_index, gu_count, down_vals, down_index, down_count
):
    tables = tables_of(gu_index, gu_count, down_index, down_count)
    units, wgu, xs, dys = front(
        tables, tokens, cotangent, gate_vals[0, 0], up_vals[0, 0], down_vals[0, 0]
    )
    d_tokens, gate_g, up_g, down_g = back(
        tables, units.reshape(512, -1), wgu, xs.reshape(512, -1), dys.reshape(512, -1), gate_vals.shape[2]
    )
    return (d_tokens, gate_g[None, None], up_g[None, None], down_g[None, None])


def solution(mesh):
    in_specs = (
        P("wide", "narrow"),
        P("wide", "narrow"),
        P("narrow", "wide", None, None, None),
        P("narrow", "wide", None, None, None),
        P("narrow", "wide", None),
        P("narrow", "wide"),
        P("wide", "narrow", None, None, None),
        P("wide", "narrow", None),
        P("wide", "narrow"),
    )
    out_specs = (
        P("wide", "narrow"),
        P("narrow", "wide", None, None, None),
        P("narrow", "wide", None, None, None),
        P("wide", "narrow", None, None, None),
    )
    return jax.shard_map(
        on_device, mesh=mesh, in_specs=in_specs, out_specs=out_specs, check_vma=False
    )
```

time: 110 us -> 110 us (level)
  local copies, waits for them, and re-layouts: 0.61 us -> 5.03 us
  Pallas kernels: 105 us -> 102 us
  other arithmetic: 1.34 us -> 0 us
    pallas_call x3 -> x2, Pallas kernels: 44.2 us -> 39.7 us  [the longest x1 38.3 us: back(): pl.pallas_call(back_kernel, out_shape=(jax.ShapeDtypeStruct((8, width), B...]
    unnamed x5 -> x8, local copies, waits for them, and re-layouts: 0.61 us -> 5.03 us
    pallas_call x1, Pallas kernels: 60.5 us -> 62.1 us  [front(): pl.pallas_call(front_kernel, out_shape=(jax.ShapeDtypeStruct((8, N, 8, 6...]
    another operation x1 -> x0, other arithmetic: 1.34 us -> none  [on_device(): units, xs, dys = front(jnp.stack([tokens, cotangent]), wgu, wd)]
where the time goes in v3:
time: 110 us; the launch traced here: 109 us
  Pallas kernels  102 us (93%)
  local copies, waits for them, and re-layouts  5.03 us (5%)
  between operations  1.95 us (2%)
    pallas_call x1, Pallas kernels, front(): pl.pallas_call(front_kernel, out_shape=(jax.ShapeDtypeStruct((8, N, 8, 6...  62.1 us
    pallas_call x1, Pallas kernels, back(): pl.pallas_call(back_kernel, out_shape=(jax.ShapeDtypeStruct((8, width), B...  38.3 us
    unnamed x8, local copies, waits for them, and re-layouts  5.03 us

profile of v3, /device:TPU:6, one launch (start us, length us, event | category | flops | bytes accessed | tf_op | source)
XLA Modules:
  0.0 108.8 jit_solution(14703391559166291428)
XLA Ops:
  1.9 1.4 %tables.1 = s32[8,16]{1,0:T(8,128)} custom-call(s32[1,1,12]{2,1,0:T(1,128)} %gu_index.1, s32[1,1]{1,0:T(1,128)S(6)} %copy.17.gu_count, s32[1,1,12]{2,1,0:T(1,128)} %down_index.1, s32[1,1]{1,0:T(1,128)S(6)} %copy.18.down_count), custom_call_target="tpu_custom_call" | custom-call | tf_op jit(solution)/shard_map/tables/pallas_call | solution.py:66
  3.3 62.1 %front.1 = (bf16[8,8,8,768]{3,2,1,0:T(8,128)(2,1)}, bf16[1024,512]{1,0:T(8,128)(2,1)}, bf16[8,64,1024]{2,1,0:T(8,128)(2,1)}, bf16[8,64,1024]{2,1,0:T(8,128)(2,1)}) custom-call(s32[8,16]{1,0:T(8,128)} %tables.1, bf16[8,1024]{1,0:T(8,128)(2,1)} %tokens.1, bf16[8,1024]{1,0:T(8,128)(2,1)} %cotangent.1, bf16[12,128,128]{2,1,0:T(8,128)(2,1)} %bitcast.15, ...), custom_call_target="tpu_custom_call" | custom-call | tf_op jit(solution)/shard_map/front/pallas_call | solution.py:236
  65.4 38.3 %back.1 = (bf16[8,1024]{1,0:T(8,128)(2,1)}, bf16[12,128,128]{2,1,0:T(8,128)(2,1)}, bf16[12,128,128]{2,1,0:T(8,128)(2,1)}, bf16[12,128,128]{2,1,0:T(8,128)(2,1)}) custom-call(s32[8,16]{1,0:T(8,128)} %tables.1, bf16[512,768]{1,0:T(8,128)(2,1)} %bitcast.11, bf16[1024,512]{1,0:T(8,128)(2,1)} %get-tuple-element.13.wgu, bf16[512,1024]{1,0:T(8,128)(2,1)} %bitcast.9, ...), custom_call_target="tpu_custom_call" | custom-call | tf_op jit(solution)/shard_map/back/pallas_call | solution.py:407
  103.8 1.3 %copy.19 = bf16[8,1024]{1,0:T(8,128)(2,1)} copy(bf16[8,1024]{1,0:T(8,128)(2,1)} %get-tuple-element.24) | data formatting | bytes 32768
  105.1 0.0 copy-start.1
  105.1 1.8 %copy.20 = bf16[1,1,12,128,128]{4,3,2,1,0:T(8,128)(2,1)} copy(bf16[1,1,12,128,128]{4,3,2,1,0:T(8,128)(2,1)} %bitcast.14) | data formatting | bytes 786432
  106.9 0.0 copy-done.1
  106.9 0.0 copy-start
  106.9 0.7 copy.21
  107.6 0.4 copy-done
  108.0 0.7 copy.22
Async XLA Ops:
  105.1 1.8 %copy-start.1 = (bf16[12,128,128]{2,1,0:T(8,128)(2,1)S(1)}, bf16[12,128,128]{2,1,0:T(8,128)(2,1)}, u32[]{:S(2)}) copy-start(bf16[12,128,128]{2,1,0:T(8,128)(2,1)} %get-tuple-element.18) | copy-start | bytes 1179652
  106.9 1.1 %copy-start = (bf16[12,128,128]{2,1,0:T(8,128)(2,1)S(1)}, bf16[12,128,128]{2,1,0:T(8,128)(2,1)}, u32[]{:S(2)}) copy-start(bf16[12,128,128]{2,1,0:T(8,128)(2,1)} %get-tuple-element.19) | copy-start | bytes 1179652

commit v4 on v3

--- a/solution.py
+++ b/solution.py
@@ -79,14 +79,18 @@
 ORDER = (4, 3, 5, 2, 6, 1, 7)
 
 
-def front_kernel(
+def layer_kernel(
     tables,
     tokens,
     cotangent,
     gate,
     up,
     down,
+    out,
+    dgu,
+    dd,
     units,
+    flat,
     wgu,
     xs,
     dys,
@@ -104,6 +108,7 @@
     s_recv,
     g_send,
     g_recv,
+    *back_refs,
 ):
     z, y, c = wide_place()
     n = lax.axis_index("narrow")
@@ -127,7 +132,7 @@
     cores = {}
     last = {}
     reduces = {}
-    shares = []
+    shares = {}
 
     def ring(s, q):
         for d in (0, 1):
@@ -162,11 +167,11 @@
             return jnp.concatenate([got[slot, which].astype(F32) for slot in slots], axis=0).astype(BF16)
 
         x = rows_of(0)
-        xs[k - 1] = x
+        xs[64 * (k - 1) : 64 * k, :] = x
         gu = jnp.dot(x, wgu[...], preferred_element_type=F32)
         part[k - 1, :, :, : 4 * B] = gu.reshape(8, 8, 4 * B)
         dy = rows_of(1)
-        dys[k - 1] = dy
+        dys[64 * (k - 1) : 64 * k, :] = dy
         dh = lax.dot_general(dy, wd[...], (((1,), (1,)), ((), ())), preferred_element_type=F32)
         part[k - 1, :, :, 4 * B :] = dh.reshape(8, 8, 2 * B)
         for j in ORDER:
@@ -192,16 +197,19 @@
         ).astype(BF16)
         units[k - 1, n, :, 4 * B :] = (d_hidden * gate * sig).astype(BF16)
         for j in ORDER:
-            shares.append(
-                send(
-                    "narrow",
-                    peers[j],
-                    units.at[k - 1, n],
-                    units.at[k - 1, n],
-                    g_send.at[k - 1, j],
-                    g_recv.at[k - 1, j],
-                )
+            shares[k, j] = send(
+                "narrow",
+                peers[j],
+                units.at[k - 1, n],
+                units.at[k - 1, n],
+                g_send.at[k - 1, j],
+                g_recv.at[k - 1, j],
             )
+
+    def settle(k):
+        for j in ORDER:
+            shares[k, j].wait_recv()
+        flat[64 * (k - 1) : 64 * k, :] = units[k - 1].astype(F32).reshape(64, -1).astype(BF16)
 
     def place(table, sources, target, width):
         for block in range(16):
@@ -223,45 +231,16 @@
             chunk(i - 3)
         if i > 4:
             finish(i - 4)
+        if i > 5:
+            settle(i - 5)
     finish(8)
-    for copy in shares:
-        copy.wait_recv()
-    for copy in sent + list(cores.values()) + list(reduces.values()) + shares:
+    settle(7)
+    settle(8)
+    back(flat, wgu, xs, dys, out, dgu, dd, *back_refs)
+    for group in (cores, reduces, shares):
+        sent.extend(group.values())
+    for copy in sent:
         copy.wait_send()
-
-
-def front(tables, tokens, cotangent, gate, up, down):
-    width = tokens.shape[-1]
-    sem = pltpu.SemaphoreType.DMA
-    return pl.pallas_call(
-        front_kernel,
-        out_shape=(
-            jax.ShapeDtypeStruct((8, N, 8, 6 * B), BF16),
-            jax.ShapeDtypeStruct((8 * B, 4 * B), BF16),
-            jax.ShapeDtypeStruct((8, 64, width), BF16),
-            jax.ShapeDtypeStruct((8, 64, width), BF16),
-        ),
-        in_specs=[SMEM] + [VMEM] * 5,
-        out_specs=(VMEM,) * 4,
-        scratch_shapes=[
-            pltpu.VMEM((2 * B, 8 * B), BF16),
-            pltpu.VMEM((4 * Z, 2, 8, width), BF16),
-            pltpu.VMEM((8, N, 8, 6 * B), F32),
-            pltpu.VMEM((8, N, 8, 6 * B), F32),
-            sem((2,)),
-            sem((2,)),
-            sem((32,)),
-            sem((32,)),
-            sem((32,)),
-            sem((32,)),
-            sem((8, N)),
-            sem((8, N)),
-            sem((8, N)),
-            sem((8, N)),
-        ],
-        compiler_params=pltpu.CompilerParams(collective_id=0, has_side_effects=True),
-        name="front",
-    )(tables, tokens, cotangent, gate, up, down)
 
 
 def chunk_of(off):
@@ -270,32 +249,12 @@
     return abs(off) - 1, (off > 0) * 1
 
 
-def back_kernel(
-    tables,
-    units,
-    wgu,
-    xs,
-    dys,
-    out,
-    gate_g,
-    up_g,
-    down_g,
-    dgu,
-    dd,
-    part,
-    held,
-    run,
-    last,
-    c_send,
-    c_recv,
-    z_send,
-    z_recv,
-    y_sem,
+def back(
+    units, wgu, xs, dys, out, dgu, dd, part, held, run, last, c_send, c_recv, z_send, z_recv, y_sem
 ):
     z, y, c = wide_place()
     right, left = wide_at(z + 1, y, c), wide_at(z - 1, y, c)
     across, partner = wide_at(z, 1 - y, c), wide_at(z, y, 1 - c)
-    greet([("wide", w) for w in (right, left, across, partner)])
     rows = (1 - y, y)
     cores = {}
 
@@ -338,13 +297,6 @@
             for row in (0, 1):
                 for col in range(4):
                     dd[8 * row + 4 * half + col] = dense[row * B : (row + 1) * B, col * B : (col + 1) * B]
-        elif s == 6:
-            for k in range(gate_g.shape[0]):
-                gate_g[k] = only_if(tables[1, k], dgu[0, tables[0, k]])
-                up_g[k] = only_if(tables[1, k], dgu[1, tables[0, k]])
-        else:
-            for k in range(down_g.shape[0]):
-                down_g[k] = only_if(tables[5, k], dd[tables[4, k]])
 
     prev = {}
     sent = []
@@ -400,18 +352,38 @@
         copy.wait_send()
 
 
-def back(tables, units, wgu, xs, dys, slots):
-    width = wgu.shape[0]
+def layer(tables, tokens, cotangent, gate, up, down):
+    width = tokens.shape[-1]
     sem = pltpu.SemaphoreType.DMA
-    grad = jax.ShapeDtypeStruct((slots, B, B), BF16)
     return pl.pallas_call(
-        back_kernel,
-        out_shape=(jax.ShapeDtypeStruct((8, width), BF16), grad, grad, grad),
-        in_specs=[SMEM] + [VMEM] * 4,
-        out_specs=(VMEM,) * 4,
+        layer_kernel,
+        out_shape=(
+            jax.ShapeDtypeStruct((8, width), BF16),
+            jax.ShapeDtypeStruct((2, 16, B, B), BF16),
+            jax.ShapeDtypeStruct((16, B, B), BF16),
+        ),
+        in_specs=[SMEM] + [VMEM] * 5,
+        out_specs=(VMEM,) * 3,
         scratch_shapes=[
-            pltpu.VMEM((2, 16, B, B), BF16),
-            pltpu.VMEM((16, B, B), BF16),
+            pltpu.VMEM((8, N, 8, 6 * B), BF16),
+            pltpu.VMEM((512, 6 * B), BF16),
+            pltpu.VMEM((8 * B, 4 * B), BF16),
+            pltpu.VMEM((512, width), BF16),
+            pltpu.VMEM((512, width), BF16),
+            pltpu.VMEM((2 * B, 8 * B), BF16),
+            pltpu.VMEM((4 * Z, 2, 8, width), BF16),
+            pltpu.VMEM((8, N, 8, 6 * B), F32),
+            pltpu.VMEM((8, N, 8, 6 * B), F32),
+            sem((2,)),
+            sem((2,)),
+            sem((32,)),
+            sem((32,)),
+            sem((32,)),
+            sem((32,)),
+            sem((8, N)),
+            sem((8, N)),
+            sem((8, N)),
+            sem((8, N)),
             pltpu.VMEM((8, 2, 2, 2, 8, width), F32),
             pltpu.VMEM((8, 2, 2, 8, width), F32),
             pltpu.VMEM((2, 2, 9, 8, width), F32),
@@ -422,21 +394,57 @@
             sem((32,)),
             sem((2,)),
         ],
-        compiler_params=pltpu.CompilerParams(collective_id=2, has_side_effects=True),
-        name="back",
-    )(tables, units, wgu, xs, dys)
+        compiler_params=pltpu.CompilerParams(collective_id=0, has_side_effects=True),
+        name="layer",
+    )(tables, tokens, cotangent, gate, up, down)
+
+
+def pick_kernel(gu_index, gu_count, down_index, down_count, mine, dgu, dd, out, gate_g, up_g, down_g):
+    out[...] = mine[...]
+    for s in range(gate_g.shape[0]):
+        alive = s < gu_count[0, 0]
+
+        @pl.when(alive)
+        def _():
+            at = gu_index[0, 0, s]
+            gate_g[s] = dgu[0, at]
+            up_g[s] = dgu[1, at]
+
+        @pl.when(jnp.logical_not(alive))
+        def _():
+            gate_g[s] = jnp.zeros((B, B), BF16)
+            up_g[s] = jnp.zeros((B, B), BF16)
+
+        d_alive = s < down_count[0, 0]
+
+        @pl.when(d_alive)
+        def _():
+            down_g[s] = dd[down_index[0, 0, s]]
+
+        @pl.when(jnp.logical_not(d_alive))
+        def _():
+            down_g[s] = jnp.zeros((B, B), BF16)
+
+
+def pick(places, mine, dgu, dd, slots):
+    grad = jax.ShapeDtypeStruct((slots, B, B), BF16)
+    return pl.pallas_call(
+        pick_kernel,
+        out_shape=(jax.ShapeDtypeStruct(mine.shape, BF16), grad, grad, grad),
+        in_specs=[SMEM] * 4 + [VMEM] * 3,
+        out_specs=(VMEM,) * 4,
+        name="pick",
+    )(*places, mine, dgu, dd)
 
 
 def on_device(
     tokens, cotangent, gate_vals, up_vals, gu_index, gu_count, down_vals, down_index, down_count
 ):
-    tables = tables_of(gu_index, gu_count, down_index, down_count)
-    units, wgu, xs, dys = front(
-        tables, tokens, cotangent, gate_vals[0, 0], up_vals[0, 0], down_vals[0, 0]
+    places = (gu_index, gu_count, down_index, down_count)
+    mine, dgu, dd = layer(
+        tables_of(*places), tokens, cotangent, gate_vals[0, 0], up_vals[0, 0], down_vals[0, 0]
     )
-    d_tokens, gate_g, up_g, down_g = back(
-        tables, units.reshape(512, -1), wgu, xs.reshape(512, -1), dys.reshape(512, -1), gate_vals.shape[2]
-    )
+    d_tokens, gate_g, up_g, down_g = pick(places, mine, dgu, dd, gate_vals.shape[2])
     return (d_tokens, gate_g[None, None], up_g[None, None], down_g[None, None])
 
 

time: 110 us -> 103 us (0.936)
  local copies, waits for them, and re-layouts: 5.03 us -> 0 us
  Pallas kernels: 102 us -> 100 us
    unnamed x8 -> x0, local copies, waits for them, and re-layouts: 5.03 us -> none
    pallas_call x2, Pallas kernels: 100 us -> 98.8 us  [the longest x1 96 us: layer(): pl.pallas_call(layer_kernel, out_shape=(jax.ShapeDtypeStruct((8, width),...]
where the time goes in v4:
time: 103 us; the launch traced here: 102 us
  Pallas kernels  100 us (97%)
  between operations  1.94 us (2%)
    pallas_call x1, Pallas kernels, layer(): pl.pallas_call(layer_kernel, out_shape=(jax.ShapeDtypeStruct((8, width),...  96 us
    pallas_call x1, Pallas kernels, pick(): pl.pallas_call(pick_kernel, out_shape=(jax.ShapeDtypeStruct(mine.shape, B...  2.78 us

profile of v4, /device:TPU:6, one launch (start us, length us, event | category | flops | bytes accessed | tf_op | source)
XLA Modules:
  0.0 102.1 jit_solution(5023230626390699745)
XLA Ops:
  1.9 1.4 %tables.1 = s32[8,16]{1,0:T(8,128)} custom-call(s32[1,1,12]{2,1,0:T(1,128)} %gu_index.3, s32[1,1]{1,0:T(1,128)S(6)} %copy.13.gu_count, s32[1,1,12]{2,1,0:T(1,128)} %down_index.3, s32[1,1]{1,0:T(1,128)S(6)} %copy.14.down_count), custom_call_target="tpu_custom_call" | custom-call | tf_op jit(solution)/shard_map/tables/pallas_call | solution.py:66
  3.3 96.0 %layer.1 = (bf16[8,1024]{1,0:T(8,128)(2,1)}, bf16[2,16,128,128]{3,2,1,0:T(8,128)(2,1)}, bf16[16,128,128]{2,1,0:T(8,128)(2,1)}) custom-call(s32[8,16]{1,0:T(8,128)} %tables.1, bf16[8,1024]{1,0:T(8,128)(2,1)} %tokens.1, bf16[8,1024]{1,0:T(8,128)(2,1)} %cotangent.1, bf16[12,128,128]{2,1,0:T(8,128)(2,1)} %bitcast.6, bf16[12,128,128]{2,1,0:T(8,128)(2,1)} %bitcast.7, ...), custom_call_target="tpu_custom_call" | custom-call | tf_op jit(solution)/shard_map/layer/pallas_call | solution.py:358
  99.4 2.8 %pick.1 = (bf16[8,1024]{1,0:T(8,128)(2,1)}, bf16[12,128,128]{2,1,0:T(8,128)(2,1)}, bf16[12,128,128]{2,1,0:T(8,128)(2,1)}, bf16[12,128,128]{2,1,0:T(8,128)(2,1)}) custom-call(s32[1,1,12]{2,1,0:T(1,128)} %gu_index.3, s32[1,1]{1,0:T(1,128)S(6)} %copy.13.gu_count, s32[1,1,12]{2,1,0:T(1,128)} %down_index.3, s32[1,1]{1,0:T(1,128)S(6)} %copy.14.down_count, ...), custom_call_target="tpu_custom_call" | custom-call | tf_op jit(solution)/shard_map/pick/pallas_call | solution.py:431

commit v5 on v4

--- a/solution.py
+++ b/solution.py
@@ -219,23 +219,23 @@
                 at = 2 * B * i + col
                 target[row : row + B, at : at + B] = only_if(flag, source[slot])
 
-    for i in range(1, 12):
+    for i in range(1, 11):
         if i <= 9:
             ring(i, 0)
         if i == 1:
             place(0, (gate, up), wgu, 2)
             place(4, (down,), wd, 8)
-        elif i <= 10:
+        else:
             ring(i - 1, 1)
+        if i > 2:
+            chunk(i - 2)
         if i > 3:
-            chunk(i - 3)
-        if i > 4:
-            finish(i - 4)
+            finish(i - 3)
         if i > 5:
             settle(i - 5)
     finish(8)
-    settle(7)
-    settle(8)
+    for k in (6, 7, 8):
+        settle(k)
     back(flat, wgu, xs, dys, out, dgu, dd, *back_refs)
     for group in (cores, reduces, shares):
         sent.extend(group.values())
@@ -333,8 +333,8 @@
             step(i - 1, 1)
         if i + 2 < 8:
             terms(i + 2)
-        if i < 8:
-            gradients(i)
+        if 2 <= i < 8:
+            gradients(i - 2)
     cores[0].wait_recv()
 
     def total(q):

time: 103 us -> 101 us (0.981); the launches traced: 102 us -> 99.1 us
  Pallas kernels: 100 us -> 97.1 us
    pallas_call x1, Pallas kernels: 96 us -> 92.9 us  [layer(): pl.pallas_call(layer_kernel, out_shape=(jax.ShapeDtypeStruct((8, width),...]
where the time goes in v5:
time: 101 us; the launch traced here: 99.1 us
  Pallas kernels  97.1 us (96%)
  between operations  1.94 us (2%)
    pallas_call x1, Pallas kernels, layer(): pl.pallas_call(layer_kernel, out_shape=(jax.ShapeDtypeStruct((8, width),...  92.9 us
    pallas_call x1, Pallas kernels, pick(): pl.pallas_call(pick_kernel, out_shape=(jax.ShapeDtypeStruct(mine.shape, B...  2.79 us

profile of v5, /device:TPU:6, one launch (start us, length us, event | category | flops | bytes accessed | tf_op | source)
XLA Modules:
  0.0 99.1 jit_solution(3491106494547668230)
XLA Ops:
  1.9 1.4 %tables.1 = s32[8,16]{1,0:T(8,128)} custom-call(s32[1,1,12]{2,1,0:T(1,128)} %gu_index.3, s32[1,1]{1,0:T(1,128)S(6)} %copy.13.gu_count, s32[1,1,12]{2,1,0:T(1,128)} %down_index.3, s32[1,1]{1,0:T(1,128)S(6)} %copy.14.down_count), custom_call_target="tpu_custom_call" | custom-call | tf_op jit(solution)/shard_map/tables/pallas_call | solution.py:66
  3.3 92.9 %layer.1 = (bf16[8,1024]{1,0:T(8,128)(2,1)}, bf16[2,16,128,128]{3,2,1,0:T(8,128)(2,1)}, bf16[16,128,128]{2,1,0:T(8,128)(2,1)}) custom-call(s32[8,16]{1,0:T(8,128)} %tables.1, bf16[8,1024]{1,0:T(8,128)(2,1)} %tokens.1, bf16[8,1024]{1,0:T(8,128)(2,1)} %cotangent.1, bf16[12,128,128]{2,1,0:T(8,128)(2,1)} %bitcast.6, bf16[12,128,128]{2,1,0:T(8,128)(2,1)} %bitcast.7, ...), custom_call_target="tpu_custom_call" | custom-call | tf_op jit(solution)/shard_map/layer/pallas_call | solution.py:358
  96.3 2.8 %pick.1 = (bf16[8,1024]{1,0:T(8,128)(2,1)}, bf16[12,128,128]{2,1,0:T(8,128)(2,1)}, bf16[12,128,128]{2,1,0:T(8,128)(2,1)}, bf16[12,128,128]{2,1,0:T(8,128)(2,1)}) custom-call(s32[1,1,12]{2,1,0:T(1,128)} %gu_index.3, s32[1,1]{1,0:T(1,128)S(6)} %copy.13.gu_count, s32[1,1,12]{2,1,0:T(1,128)} %down_index.3, s32[1,1]{1,0:T(1,128)S(6)} %copy.14.down_count, ...), custom_call_target="tpu_custom_call" | custom-call | tf_op jit(solution)/shard_map/pick/pallas_call | solution.py:431

commit v6 on v5

--- a/solution.py
+++ b/solution.py
@@ -229,12 +229,13 @@
             ring(i - 1, 1)
         if i > 2:
             chunk(i - 2)
-        if i > 3:
-            finish(i - 3)
-        if i > 5:
-            settle(i - 5)
+        if i > 4:
+            finish(i - 4)
+        if i > 6:
+            settle(i - 6)
+    finish(7)
     finish(8)
-    for k in (6, 7, 8):
+    for k in (5, 6, 7, 8):
         settle(k)
     back(flat, wgu, xs, dys, out, dgu, dd, *back_refs)
     for group in (cores, reduces, shares):

time: 101 us -> 98.8 us (0.978)
  Pallas kernels: 97.1 us -> 95.4 us
    pallas_call x1, Pallas kernels: 92.9 us -> 91.2 us  [layer(): pl.pallas_call(layer_kernel, out_shape=(jax.ShapeDtypeStruct((8, width),...]
where the time goes in v6:
time: 98.8 us; the launch traced here: 97.3 us
  Pallas kernels  95.4 us (97%)
  between operations  1.94 us (2%)
    pallas_call x1, Pallas kernels, layer(): pl.pallas_call(layer_kernel, out_shape=(jax.ShapeDtypeStruct((8, width),...  91.2 us
    pallas_call x1, Pallas kernels, pick(): pl.pallas_call(pick_kernel, out_shape=(jax.ShapeDtypeStruct(mine.shape, B...  2.79 us

profile of v6, /device:TPU:6, one launch (start us, length us, event | category | flops | bytes accessed | tf_op | source)
XLA Modules:
  0.0 97.3 jit_solution(15538549955479880262)
XLA Ops:
  1.9 1.4 %tables.1 = s32[8,16]{1,0:T(8,128)} custom-call(s32[1,1,12]{2,1,0:T(1,128)} %gu_index.3, s32[1,1]{1,0:T(1,128)S(6)} %copy.13.gu_count, s32[1,1,12]{2,1,0:T(1,128)} %down_index.3, s32[1,1]{1,0:T(1,128)S(6)} %copy.14.down_count), custom_call_target="tpu_custom_call" | custom-call | tf_op jit(solution)/shard_map/tables/pallas_call | solution.py:66
  3.3 91.2 %layer.1 = (bf16[8,1024]{1,0:T(8,128)(2,1)}, bf16[2,16,128,128]{3,2,1,0:T(8,128)(2,1)}, bf16[16,128,128]{2,1,0:T(8,128)(2,1)}) custom-call(s32[8,16]{1,0:T(8,128)} %tables.1, bf16[8,1024]{1,0:T(8,128)(2,1)} %tokens.1, bf16[8,1024]{1,0:T(8,128)(2,1)} %cotangent.1, bf16[12,128,128]{2,1,0:T(8,128)(2,1)} %bitcast.6, bf16[12,128,128]{2,1,0:T(8,128)(2,1)} %bitcast.7, ...), custom_call_target="tpu_custom_call" | custom-call | tf_op jit(solution)/shard_map/layer/pallas_call | solution.py:359
  94.5 2.8 %pick.1 = (bf16[8,1024]{1,0:T(8,128)(2,1)}, bf16[12,128,128]{2,1,0:T(8,128)(2,1)}, bf16[12,128,128]{2,1,0:T(8,128)(2,1)}, bf16[12,128,128]{2,1,0:T(8,128)(2,1)}) custom-call(s32[1,1,12]{2,1,0:T(1,128)} %gu_index.3, s32[1,1]{1,0:T(1,128)S(6)} %copy.13.gu_count, s32[1,1,12]{2,1,0:T(1,128)} %down_index.3, s32[1,1]{1,0:T(1,128)S(6)} %copy.14.down_count, ...), custom_call_target="tpu_custom_call" | custom-call | tf_op jit(solution)/shard_map/pick/pallas_call | solution.py:432
